TPU v7x, 256 devices: a whole 4x4x8 slice. The times are simulated.
256 devices in a mesh: row: 8 (over x, core), col: 32 (over y, z).
Axes of the slice: x: 4, y: 4, z: 8, core: 2. Of those that a mesh axis runs over, the one named last changes fastest.
Arguments:
- affinity_tiles: bfloat16 [1024, 64, 128, 128], P(('row', 'col'))
- block_columns: int32 [1024, 64], P(('row', 'col')), may hold values from 0 to 127, as said below
- live_counts: int32 [8, 128], P('row', 'col'), may hold values from 1 to 64, 4096 in all within a row
- earlier_blocks: float32 [4, 64, 131072], P(None, None, ('row', 'col')), may hold values from -6 to 6
Outputs:
- new_blocks: float32 [2, 64, 131072], P(None, None, ('row', 'col'))
- triangular_factors: float32 [2, 64, 64], replicated
Inputs may be any that keep to these rules, and one draw needn't show every extreme that they name: `block_columns`: slot 0 of every block row names the block row itself; columns name block rows of the same row group. `live_counts`: slots at or past a block row's count are ignored.
All inputs are finite; a program needn't handle non-finite values.
Results may differ from a plain program's by a relative error of at most 0.0059.
Values may be sent and summed in bfloat16 or wider, within the bound.
No kernel may reach another device: no remote copies, remote signals or barrier semaphores. Data moves between devices by JAX's collectives and lax.ppermute only.
A program may use at most 64 MiB of HBM per device.

v0:
```python
import jax
import jax.numpy as jnp
from jax import lax
from jax.sharding import PartitionSpec as P

STEPS = 2


def apply_tiles(affinity_tiles, block_columns, row_counts, group_blocks):
    block_rows = affinity_tiles.shape[0]
    slot_count = affinity_tiles.shape[1]
    tile_size = affinity_tiles.shape[2]
    block_width = group_blocks.shape[0]
    slot_ids = lax.broadcasted_iota(jnp.int32, (block_rows, slot_count), 1)
    live_mask = slot_ids < row_counts[:, None]
    picked = jnp.take(group_blocks, block_columns, axis=1)
    picked = jnp.where(live_mask[None, :, :, None], picked, jnp.zeros((), jnp.bfloat16))
    running = jnp.einsum(
        "rsij,brsj->bri", affinity_tiles, picked, preferred_element_type=jnp.float32
    )
    return running.reshape(block_width, block_rows * tile_size)


def on_device(affinity_tiles, block_columns, live_counts, earlier_blocks):
    block_rows = affinity_tiles.shape[0]
    tile_size = affinity_tiles.shape[2]
    block_width = earlier_blocks.shape[1]
    rows_here = earlier_blocks.shape[2]
    total_rows = rows_here * lax.axis_size("row") * lax.axis_size("col")
    row_counts = live_counts.reshape(block_rows)
    known_list = [earlier_blocks[i] for i in range(earlier_blocks.shape[0])]
    first_half = known_list[-1].astype(jnp.bfloat16)
    group_half = lax.all_gather(first_half, "col", axis=1, tiled=True)
    fresh_list = []
    factor_list = []
    for step_index in range(STEPS):
        is_last = step_index + 1 == STEPS
        group_blocks = group_half.reshape(block_width, -1, tile_size)
        product = apply_tiles(affinity_tiles, block_columns, row_counts, group_blocks)
        known = jnp.concatenate(known_list, 0)
        local_proj = jnp.dot(known, product.T, precision=lax.Precision.HIGHEST) / total_rows
        projections = lax.psum(local_proj, ("row", "col"))
        residual = product - jnp.dot(projections.T, known, precision=lax.Precision.HIGHEST)
        local_gram = jnp.dot(residual, residual.T, precision=lax.Precision.HIGHEST) / total_rows
        gram_sum = lax.psum(local_gram, ("row", "col"))
        factor_low = jnp.linalg.cholesky(gram_sum)
        fresh = jax.scipy.linalg.solve_triangular(factor_low, residual, lower=True)
        fresh_list.append(fresh)
        factor_list.append(factor_low.T)
        known_list.append(fresh)
        if not is_last:
            group_half = lax.all_gather(fresh.astype(jnp.bfloat16), "col", axis=1, tiled=True)
    return (jnp.stack(fresh_list), jnp.stack(factor_list))


def solution(mesh):
    return jax.shard_map(
        on_device,
        mesh=mesh,
        in_specs=(
            P(("row", "col"), None, None, None),
            P(("row", "col"), None),
            P("row", "col"),
            P(None, None, ("row", "col")),
        ),
        out_specs=(P(None, None, ("row", "col")), P()),
        check_vma=False,
    )
```

profile of v0, /device:TPU:1, one launch (start us, length us, event | category | flops | bytes accessed | tf_op | source)
XLA Modules:
  0.0 864.7 jit_solution(17645085274301516106)
XLA Ops:
  7.2 1.5 fusion.32
  11.3 0.9 constant_dynamic-update-slice_fusion.3
  13.1 1.1 slice_bitcast_fusion.2
  14.3 71.6 %all-gather.3.cloned.1.call-done = bf16[64,16384]{1,0:T(8,128)(2,1)} async-done(((bf16[64,512]{1,0:T(8,128)(2,1)}), bf16[64,16384]{1,0:T(8,128)(2,1)}) %all-gather.3.cloned.1.call-update) | async-done | bytes 2097168 | tf_op jit(solution)/shard_map/all_gather | solution.py:33
  85.9 2.2 copy_bitcast_fusion.1
  88.1 3.0 gather_fusion
  91.1 6.3 fusion.12
  97.3 1.2 convolution_multiply_fusion.1
  99.6 246.5 %all-reduce.3.cloned.1.call-done = f32[256,64]{1,0:T(8,128)} async-done(((f32[256,64]{1,0:T(8,128)}), f32[256,64]{1,0:T(8,128)}) %all-reduce.3.cloned.1.call-update) | async-done | bytes 65552 | tf_op jit(solution)/shard_map/psum | solution.py:42
  346.0 1.3 convolution_subtract_fusion.1
  347.6 76.2 %psum.29 = f32[64,64]{0,1:T(8,128)S(1)} all-reduce(f32[64,64]{0,1:T(8,128)S(1)} %convolution_multiply_fusion.3), channel_id=1, replica_groups=mesh['row'=8,'col'=32] {'row','col'}, use_global_device_ids=true, to_apply=%region_1.3 | all-reduce | flops 4096 | bytes 32768 | tf_op jit(solution)/shard_map/psum | solution.py:45
  423.9 5.8 cholesky.44
  431.1 4.9 custom-call.6
  436.0 1.0 fusion.33
  437.0 66.8 %all-gather.5.cloned.1.call-done = bf16[64,16384]{1,0:T(8,128)(2,1)} async-done(((bf16[64,512]{1,0:T(8,128)(2,1)}), bf16[64,16384]{1,0:T(8,128)(2,1)}) %all-gather.5.cloned.1.call-update) | async-done | bytes 2097168 | tf_op jit(solution)/shard_map/all_gather | solution.py:52
  503.8 2.2 copy_bitcast_fusion
  506.0 3.0 gather_fusion.1
  509.0 6.3 fusion.13
  515.3 1.3 convolution_multiply_fusion
  516.7 251.0 %all-reduce.5.cloned.1.call-done = f32[320,64]{1,0:T(8,128)} async-done(((f32[320,64]{1,0:T(8,128)}), f32[320,64]{1,0:T(8,128)}) %all-reduce.5.cloned.1.call-update) | async-done | bytes 81936 | tf_op jit(solution)/shard_map/psum | solution.py:42
  767.7 1.5 convolution_subtract_fusion
  769.4 74.8 %psum.31 = f32[64,64]{0,1:T(8,128)S(1)} all-reduce(f32[64,64]{0,1:T(8,128)S(1)} %convolution_multiply_fusion.2), channel_id=1, replica_groups=mesh['row'=8,'col'=32] {'row','col'}, use_global_device_ids=true, to_apply=%region_5.9 | all-reduce | flops 4096 | bytes 32768 | tf_op jit(solution)/shard_map/psum | solution.py:45
  844.3 5.8 cholesky.55
  852.2 4.9 custom-call.7
  (31 shorter events, 9.6 us)
Async XLA Ops:
  7.2 78.7 %all-gather.3.cloned.1.call-start = ((), (), s32[]{:S(2)}) async-start(), calls=%async_computation | async-start | bytes 2162688 | tf_op jit(solution)/shard_map/all_gather | solution.py:33
  8.8 337.2 %all-reduce.3.cloned.1.call-start = ((), (), s32[]{:S(2)}) async-start(), calls=%async_computation.1 | async-start | bytes 262144 | tf_op jit(solution)/shard_map/psum | solution.py:42
  98.6 405.2 %all-gather.5.cloned.1.call-start = ((), (), s32[]{:S(2)}) async-start(), calls=%async_computation.2 | async-start | bytes 2162688 | tf_op jit(solution)/shard_map/all_gather | solution.py:52
  437.0 330.7 %all-reduce.5.cloned.1.call-start = ((), (), s32[]{:S(2)}) async-start(), calls=%async_computation.3 | async-start | bytes 327680 | tf_op jit(solution)/shard_map/psum | solution.py:42
Sparse Core Ops, SparseCore 0:
  11.0 74.8 all-gather.2
  98.7 247.2 all-reduce.2
  437.1 66.6 all-gather.4
  516.8 250.8 all-reduce.4
where the time goes:
time: 865 us
  waiting for transfers between devices  636 us (74%)
  blocking collectives  151 us (17%)
  other arithmetic  26.4 us (3%)
  matrix products  19.7 us (2%)
  local copies, waits for them, and re-layouts  17.7 us (2%)
  between operations  13.9 us (2%)
    psum x2, waiting for transfers between devices, on_device(): projections = lax.psum(local_proj, ('row', 'col'))  497 us
    psum x2, blocking collectives, on_device(): gram_sum = lax.psum(local_gram, ('row', 'col'))  151 us
    all_gather x1, waiting for transfers between devices, on_device(): group_half = lax.all_gather(first_half, 'col', axis=1, tiled=True)  71.6 us
    all_gather x1, waiting for transfers between devices, on_device(): lax.all_gather(fresh.astype(jnp.bfloat16), 'col', axis=1, tiled=True)  66.8 us
  transfers between devices with their start and end apart: 4, of which 4 were waited for; matrix products, arithmetic and copies ran while one was open for 1% of the time, Pallas kernels for 0%

commit v1 on v0

--- a/solution.py
+++ b/solution.py
@@ -39,7 +39,7 @@
         product = apply_tiles(affinity_tiles, block_columns, row_counts, group_blocks)
         known = jnp.concatenate(known_list, 0)
         local_proj = jnp.dot(known, product.T, precision=lax.Precision.HIGHEST) / total_rows
-        projections = lax.psum(local_proj, ("row", "col"))
+        projections = lax.psum(lax.psum(local_proj, "row"), "col")
         residual = product - jnp.dot(projections.T, known, precision=lax.Precision.HIGHEST)
         local_gram = jnp.dot(residual, residual.T, precision=lax.Precision.HIGHEST) / total_rows
         gram_sum = lax.psum(local_gram, ("row", "col"))

time: 865 us -> 791 us (0.914)
  waiting for transfers between devices: 636 us -> 557 us
    psum x2 -> x4, waiting for transfers between devices: 497 us -> 417 us  [on_device(): projections = lax.psum(lax.psum(local_proj, 'row'), 'col')]
  transfers between devices with their start and end apart: 4 -> 6, of which waited for: 4 -> 6; matrix products, arithmetic and copies ran while one was open for 1% -> 1% of each run, Pallas kernels for 0% -> 0%
where the time goes in v1:
time: 791 us
  waiting for transfers between devices  557 us (70%)
  blocking collectives  157 us (20%)
  other arithmetic  26.4 us (3%)
  matrix products  19.7 us (2%)
  local copies, waits for them, and re-layouts  15.9 us (2%)
  between operations  14.3 us (2%)
    psum x4, waiting for transfers between devices, on_device(): projections = lax.psum(lax.psum(local_proj, 'row'), 'col')  417 us
    psum x2, blocking collectives, on_device(): gram_sum = lax.psum(local_gram, ('row', 'col'))  157 us
    all_gather x1, waiting for transfers between devices, on_device(): group_half = lax.all_gather(first_half, 'col', axis=1, tiled=True)  72.5 us
    all_gather x1, waiting for transfers between devices, on_device(): lax.all_gather(fresh.astype(jnp.bfloat16), 'col', axis=1, tiled=True)  67.5 us
  transfers between devices with their start and end apart: 6, of which 6 were waited for; matrix products, arithmetic and copies ran while one was open for 1% of the time, Pallas kernels for 0%

profile of v1, /device:TPU:1, one launch (start us, length us, event | category | flops | bytes accessed | tf_op | source)
XLA Modules:
  0.0 791.0 jit_solution(10278536077870864292)
XLA Ops:
  7.2 1.5 fusion.32
  12.2 1.1 slice_bitcast_fusion.2
  13.4 72.5 %all-gather.3.cloned.1.call-done = bf16[64,16384]{1,0:T(8,128)(2,1)} async-done(((bf16[64,512]{1,0:T(8,128)(2,1)}), bf16[64,16384]{1,0:T(8,128)(2,1)}) %all-gather.3.cloned.1.call-update) | async-done | bytes 2097168 | tf_op jit(solution)/shard_map/all_gather | solution.py:33
  85.9 2.2 copy_bitcast_fusion.1
  88.1 3.0 gather_fusion
  91.1 6.3 fusion.12
  97.4 1.2 convolution_multiply_fusion.1
  98.7 65.6 %all-reduce.5.cloned.1.call-done = f32[256,64]{1,0:T(8,128)} async-done(((f32[256,64]{1,0:T(8,128)}), f32[256,64]{1,0:T(8,128)}) %all-reduce.5.cloned.1.call-update) | async-done | bytes 65552 | tf_op jit(solution)/shard_map/psum | solution.py:42
  164.4 142.8 %all-reduce.7.cloned.1.call-done = f32[256,64]{1,0:T(8,128)} async-done(((f32[256,64]{1,0:T(8,128)}), f32[256,64]{1,0:T(8,128)}) %all-reduce.7.cloned.1.call-update) | async-done | bytes 65552 | tf_op jit(solution)/shard_map/psum | solution.py:42
  307.2 1.3 convolution_subtract_fusion.1
  308.7 78.2 %psum.44 = f32[64,64]{0,1:T(8,128)S(1)} all-reduce(f32[64,64]{0,1:T(8,128)S(1)} %convolution_multiply_fusion.3), channel_id=1, replica_groups=mesh['row'=8,'col'=32] {'row','col'}, use_global_device_ids=true, to_apply=%region_2.4 | all-reduce | flops 4096 | bytes 32768 | tf_op jit(solution)/shard_map/psum | solution.py:45
  387.0 5.8 cholesky.44
  394.2 4.9 custom-call.6
  400.1 67.5 %all-gather.5.cloned.1.call-done = bf16[64,16384]{1,0:T(8,128)(2,1)} async-done(((bf16[64,512]{1,0:T(8,128)(2,1)}), bf16[64,16384]{1,0:T(8,128)(2,1)}) %all-gather.5.cloned.1.call-update) | async-done | bytes 2097168 | tf_op jit(solution)/shard_map/all_gather | solution.py:52
  467.6 2.2 copy_bitcast_fusion
  469.8 3.0 gather_fusion.1
  472.8 6.3 fusion.13
  479.1 1.3 convolution_multiply_fusion
  480.5 65.9 %all-reduce.9.cloned.1.call-done = f32[320,64]{1,0:T(8,128)} async-done(((f32[320,64]{1,0:T(8,128)}), f32[320,64]{1,0:T(8,128)}) %all-reduce.9.cloned.1.call-update) | async-done | bytes 81936 | tf_op jit(solution)/shard_map/psum | solution.py:42
  546.5 142.8 %all-reduce.11.cloned.1.call-done = f32[320,64]{1,0:T(8,128)} async-done(((f32[320,64]{1,0:T(8,128)}), f32[320,64]{1,0:T(8,128)}) %all-reduce.11.cloned.1.call-update) | async-done | bytes 81936 | tf_op jit(solution)/shard_map/psum | solution.py:42
  689.3 1.5 convolution_subtract_fusion
  691.1 79.1 %psum.47 = f32[64,64]{0,1:T(8,128)S(1)} all-reduce(f32[64,64]{0,1:T(8,128)S(1)} %convolution_multiply_fusion.2), channel_id=1, replica_groups=mesh['row'=8,'col'=32] {'row','col'}, use_global_device_ids=true, to_apply=%region_7.11 | all-reduce | flops 4096 | bytes 32768 | tf_op jit(solution)/shard_map/psum | solution.py:45
  770.2 5.8 cholesky.55
  778.1 4.9 custom-call.7
  (39 shorter events, 9.8 us)
Async XLA Ops:
  7.2 78.7 %all-gather.3.cloned.1.call-start = ((), (), s32[]{:S(2)}) async-start(), calls=%async_computation | async-start | bytes 2162688 | tf_op jit(solution)/shard_map/all_gather | solution.py:33
  8.8 155.5 %all-reduce.5.cloned.1.call-start = ((), (), s32[]{:S(2)}) async-start(), calls=%async_computation.1 | async-start | bytes 262144 | tf_op jit(solution)/shard_map/psum | solution.py:42
  91.1 7.6 copy-start
  98.6 208.5 %all-reduce.7.cloned.1.call-start = ((), (), s32[]{:S(2)}) async-start(), calls=%async_computation.2 | async-start | bytes 262144 | tf_op jit(solution)/shard_map/psum | solution.py:42
  164.3 303.3 %all-gather.5.cloned.1.call-start = ((), (), s32[]{:S(2)}) async-start(), calls=%async_computation.3 | async-start | bytes 2162688 | tf_op jit(solution)/shard_map/all_gather | solution.py:52
  400.1 146.4 %all-reduce.9.cloned.1.call-start = ((), (), s32[]{:S(2)}) async-start(), calls=%async_computation.4 | async-start | bytes 327680 | tf_op jit(solution)/shard_map/psum | solution.py:42
  480.5 208.9 %all-reduce.11.cloned.1.call-start = ((), (), s32[]{:S(2)}) async-start(), calls=%async_computation.5 | async-start | bytes 327680 | tf_op jit(solution)/shard_map/psum | solution.py:42
Sparse Core Ops, SparseCore 0:
  11.0 74.8 all-gather.2
  98.8 65.4 all-reduce.4
  167.8 139.3 all-reduce.6
  400.2 67.3 all-gather.4
  480.6 65.8 all-reduce.8
  549.8 139.5 all-reduce.10
